TPU v7x, 512 devices: a whole 4x4x16 slice. The times are simulated.
512 devices in a mesh: mem: 32 (over z, core), space: 16 (over y, x).
Axes of the slice: x: 4, y: 4, z: 16, core: 2. Of those that a mesh axis runs over, the one named last changes fastest.
Arguments:
- ensemble: bfloat16 [1024, 262144], P('mem', 'space'), may hold values from -420 to 420, as said below
- log_weights: float32 [1024], replicated, may hold values from -405 to -195, as said below
Outputs:
- analysis: bfloat16 [1024, 262144], P('mem', 'space')
Inputs may be any that keep to these rules, and one draw needn't show every extreme that they name: `ensemble`: finite values. `log_weights`: unnormalized log-likelihoods; only differences between members matter.
All inputs are finite; a program needn't handle non-finite values.
Results may differ from a plain program's by a relative error of at most 0.003.
The roundings to bfloat16 on the way count: a program that leaves them out, or rounds other values in their place, can miss the bound.
Values may be sent and summed in bfloat16 or wider, within the bound.
No kernel may reach another device: no remote copies, remote signals or barrier semaphores. Data moves between devices by JAX's collectives and lax.ppermute only.
A program may use at most 64 MiB of HBM per device.

v0:
```python
import jax
import jax.numpy as jnp
from jax import lax
from jax.sharding import PartitionSpec as P

M = 1024
ITERS = 10


def coupling_from(kernel_part, weights_part, total_sum):

    def sweep(step, carry):
        row_scale, col_scale = carry
        row_scale = weights_part / jnp.dot(kernel_part, col_scale, precision=lax.Precision.HIGHEST)
        sums = total_sum(jnp.dot(row_scale, kernel_part, precision=lax.Precision.HIGHEST))
        return (row_scale, 1.0 / M / sums)

    start_col = jnp.ones((kernel_part.shape[1],), jnp.float32)
    row_scale, col_scale = lax.fori_loop(0, ITERS, sweep, (weights_part, start_col))
    return (M * row_scale[:, None] * kernel_part * col_scale[None, :]).astype(jnp.bfloat16)


def per_device(ensemble, log_weights):
    members_dev = ensemble.shape[0]
    cells_total = ensemble.shape[1] * lax.axis_size("space")
    relaid = lax.all_to_all(ensemble, "mem", split_axis=1, concat_axis=0, tiled=True)
    partial_gram = lax.dot_general(
        relaid, relaid, (((1,), (1,)), ((), ())), preferred_element_type=jnp.float32
    )
    weights = jax.nn.softmax(log_weights)
    local_rows = lax.psum_scatter(partial_gram, "mem", scatter_dimension=0, tiled=True)
    gram_rows = lax.psum(local_rows, "space")
    start = lax.axis_index("mem") * members_dev
    own_block = lax.dynamic_slice_in_dim(gram_rows, start, members_dev, 1)
    own_norms = jnp.sum(own_block * jnp.eye(members_dev, dtype=jnp.float32), axis=1)
    all_norms = lax.all_gather(own_norms, "mem", axis=0, tiled=True)
    dist = (own_norms[:, None] + all_norms[None, :] - 2.0 * gram_rows) / cells_total
    dist_total = lax.psum(jnp.sum(dist), "mem")
    mean_dist = dist_total / (M * (M - 1))
    kernel = jnp.exp(-dist / (0.08 * mean_dist))
    weights_rows = lax.dynamic_slice_in_dim(weights, start, members_dev, 0)

    def column_total(values):
        return lax.psum(values, "mem")

    coupling_rows = coupling_from(kernel, weights_rows, column_total)
    coupling = lax.all_gather(coupling_rows, "mem", axis=0, tiled=True)
    mixed = lax.dot_general(
        coupling, relaid, (((0,), (0,)), ((), ())), preferred_element_type=jnp.float32
    )
    mixed = mixed.astype(jnp.bfloat16)
    return lax.all_to_all(mixed, "mem", split_axis=0, concat_axis=1, tiled=True)


def solution(mesh):
    return jax.shard_map(
        per_device,
        mesh=mesh,
        in_specs=(P("mem", "space"), P()),
        out_specs=P("mem", "space"),
        check_vma=False,
    )
```

profile of v0, /device:TPU:1, one launch (start us, length us, event | category | flops | bytes accessed | tf_op | source)
XLA Modules:
  0.0 1010.4 jit_solution(11346003454657286297)
XLA Ops:
  6.5 1.4 copy.12
  7.9 72.3 %all_to_all.38 = bf16[32,32,512]{2,0,1:T(8,128)(2,1)S(1)} all-to-all(bf16[32,32,512]{2,0,1:T(8,128)(2,1)S(1)} %bitcast.43), channel_id=1, replica_groups=mesh['mem'=32,'space'=16] {'mem'}, dimensions={1} | all-to-all | bytes 2097152 | tf_op jit(solution)/shard_map/all_to_all | solution.py:26
  80.2 3.2 fusion.6
  83.5 1.3 dynamic-slice
  85.3 0.6 reduce_max.9
  85.9 1.2 fusion.5
  87.2 98.8 %reduce-scatter.2.cloned.1.call-done = f32[32,1024]{1,0:T(8,128)} async-done(((f32[1024,1024]{1,0:T(8,128)}), f32[32,1024]{1,0:T(8,128)}) %reduce-scatter.2.cloned.1.call-update) | async-done | bytes 131088 | tf_op jit(solution)/shard_map/reduce_scatter | solution.py:31
  186.1 1.2 fusion.4
  187.4 114.0 %all-reduce.3.cloned.1.call-done = f32[32,1024]{1,0:T(8,128)} async-done(((f32[32,1024]{1,0:T(8,128)}), f32[32,1024]{1,0:T(8,128)}) %all-reduce.3.cloned.1.call-update) | async-done | bytes 131088 | tf_op jit(solution)/shard_map/psum | solution.py:32
  301.4 1.0 select_reduce_fusion
  302.4 0.2 dynamic-update-slice
  302.7 48.6 %all-reduce = f32[1024]{0:T(1024)S(1)} all-reduce(f32[1024]{0:T(1024)S(1)} %dynamic-update-slice), channel_id=1, replica_groups=mesh['mem'=32,'space'=16] {'mem'}, use_global_device_ids=true, to_apply=%add | all-reduce | flops 1024 | bytes 8192
  351.2 1.7 fusion.3
  352.9 0.5 copy.16
  353.4 47.1 %psum.22 = f32[]{:T(128)} all-reduce(f32[]{:T(128)} %fusion.3), channel_id=1, replica_groups=mesh['mem'=32,'space'=16] {'mem'}, use_global_device_ids=true, to_apply=%region_6.0 | all-reduce | flops 1 | bytes 8 | tf_op jit(solution)/shard_map/psum | solution.py:38
  401.2 1.0 divide_exponential_fusion
  402.2 462.6 %while.13 = (s32[]{:T(128)}, f32[32]{0:T(128)}, f32[1024]{0:T(1024)S(1)}, f32[32,1024]{1,0:T(8,128)S(1)}, f32[32]{0:T(128)S(1)}, /*index=5*/s32[]{:T(128)}, s32[]{:T(128)}) while((s32[]{:T(128)}, f32[32]{0:T(128)}, f32[1024]{0:T(1024)S(1)}, f32[32,1024]{1,0:T(8,128)S(1)}, f32[32]{0:T(128)S(1)}, /*index=5*/s32[]{:T(128)}, ...), condition=%wide.region_9.0_spmd.clone, body=%wide.region_7.0_spmd.clone.sunk | while | flops 789539 | bytes 295923 | solution.py:19
  402.2 0.2 fusion.24
  402.4 0.2 fusion.25
  402.6 45.8 %psum.25 = f32[1024]{0:T(1024)S(1)} all-reduce(f32[1024]{0:T(1024)S(1)} %bitcast.49), channel_id=1, replica_groups=mesh['mem'=32,'space'=16] {'mem'}, use_global_device_ids=true, to_apply=%region_8.0 | all-reduce | flops 1024 | bytes 8192 | tf_op jit(solution)/shard_map/while/body/eval_jaxpr/psum | solution.py:44
  448.5 0.2 fusion.24
  448.7 0.2 fusion.25
  448.9 45.8 %psum.25 = f32[1024]{0:T(1024)S(1)} all-reduce(f32[1024]{0:T(1024)S(1)} %bitcast.49), channel_id=1, replica_groups=mesh['mem'=32,'space'=16] {'mem'}, use_global_device_ids=true, to_apply=%region_8.0 | all-reduce | flops 1024 | bytes 8192 | tf_op jit(solution)/shard_map/while/body/eval_jaxpr/psum | solution.py:44
  494.7 0.2 fusion.24
  494.9 0.2 fusion.25
  495.2 45.8 %psum.25 = f32[1024]{0:T(1024)S(1)} all-reduce(f32[1024]{0:T(1024)S(1)} %bitcast.49), channel_id=1, replica_groups=mesh['mem'=32,'space'=16] {'mem'}, use_global_device_ids=true, to_apply=%region_8.0 | all-reduce | flops 1024 | bytes 8192 | tf_op jit(solution)/shard_map/while/body/eval_jaxpr/psum | solution.py:44
  541.0 0.2 fusion.24
  541.2 0.2 fusion.25
  541.4 45.8 %psum.25 = f32[1024]{0:T(1024)S(1)} all-reduce(f32[1024]{0:T(1024)S(1)} %bitcast.49), channel_id=1, replica_groups=mesh['mem'=32,'space'=16] {'mem'}, use_global_device_ids=true, to_apply=%region_8.0 | all-reduce | flops 1024 | bytes 8192 | tf_op jit(solution)/shard_map/while/body/eval_jaxpr/psum | solution.py:44
  587.3 0.2 fusion.24
  587.4 0.2 fusion.25
  587.7 45.8 %psum.25 = f32[1024]{0:T(1024)S(1)} all-reduce(f32[1024]{0:T(1024)S(1)} %bitcast.49), channel_id=1, replica_groups=mesh['mem'=32,'space'=16] {'mem'}, use_global_device_ids=true, to_apply=%region_8.0 | all-reduce | flops 1024 | bytes 8192 | tf_op jit(solution)/shard_map/while/body/eval_jaxpr/psum | solution.py:44
  633.7 0.2 fusion.25
  633.9 45.8 %psum.25 = f32[1024]{0:T(1024)S(1)} all-reduce(f32[1024]{0:T(1024)S(1)} %bitcast.49), channel_id=1, replica_groups=mesh['mem'=32,'space'=16] {'mem'}, use_global_device_ids=true, to_apply=%region_8.0 | all-reduce | flops 1024 | bytes 8192 | tf_op jit(solution)/shard_map/while/body/eval_jaxpr/psum | solution.py:44
  680.0 0.2 fusion.25
  680.2 45.8 %psum.25 = f32[1024]{0:T(1024)S(1)} all-reduce(f32[1024]{0:T(1024)S(1)} %bitcast.49), channel_id=1, replica_groups=mesh['mem'=32,'space'=16] {'mem'}, use_global_device_ids=true, to_apply=%region_8.0 | all-reduce | flops 1024 | bytes 8192 | tf_op jit(solution)/shard_map/while/body/eval_jaxpr/psum | solution.py:44
  726.2 0.2 fusion.25
  726.5 45.8 %psum.25 = f32[1024]{0:T(1024)S(1)} all-reduce(f32[1024]{0:T(1024)S(1)} %bitcast.49), channel_id=1, replica_groups=mesh['mem'=32,'space'=16] {'mem'}, use_global_device_ids=true, to_apply=%region_8.0 | all-reduce | flops 1024 | bytes 8192 | tf_op jit(solution)/shard_map/while/body/eval_jaxpr/psum | solution.py:44
  772.5 0.2 fusion.25
  772.7 45.8 %psum.25 = f32[1024]{0:T(1024)S(1)} all-reduce(f32[1024]{0:T(1024)S(1)} %bitcast.49), channel_id=1, replica_groups=mesh['mem'=32,'space'=16] {'mem'}, use_global_device_ids=true, to_apply=%region_8.0 | all-reduce | flops 1024 | bytes 8192 | tf_op jit(solution)/shard_map/while/body/eval_jaxpr/psum | solution.py:44
  818.7 0.2 fusion.25
  819.0 45.8 %psum.25 = f32[1024]{0:T(1024)S(1)} all-reduce(f32[1024]{0:T(1024)S(1)} %bitcast.49), channel_id=1, replica_groups=mesh['mem'=32,'space'=16] {'mem'}, use_global_device_ids=true, to_apply=%region_8.0 | all-reduce | flops 1024 | bytes 8192 | tf_op jit(solution)/shard_map/while/body/eval_jaxpr/psum | solution.py:44
  864.8 0.6 broadcast_multiply_fusion
  865.4 0.7 multiply_convert_fusion
  866.2 70.0 %all-gather.2.cloned.1.call-done = bf16[1024,1024]{1,0:T(8,128)(2,1)} async-done(((bf16[32,1024]{1,0:T(8,128)(2,1)}), bf16[1024,1024]{1,0:T(8,128)(2,1)}) %all-gather.2.cloned.1.call-update) | async-done | bytes 2097168 | tf_op jit(solution)/shard_map/all_gather | solution.py:47
  936.2 2.9 convolution_convert_fusion
  939.0 63.8 %all_to_all.39 = bf16[32,32,512]{2,1,0:T(8,128)(2,1)S(1)} all-to-all(bf16[32,32,512]{2,1,0:T(8,128)(2,1)S(1)} %bitcast.47), channel_id=1, replica_groups=mesh['mem'=32,'space'=16] {'mem'}, dimensions={0} | all-to-all | bytes 2097152 | tf_op jit(solution)/shard_map/all_to_all | solution.py:52
  1002.8 1.1 copy.10
  (58 shorter events, 1.3 us)
Async XLA Ops:
  6.5 179.5 %reduce-scatter.2.cloned.1.call-start = ((), (), s32[]{:S(2)}) async-start(), calls=%async_computation.3 | async-start | bytes 4325376 | tf_op jit(solution)/shard_map/reduce_scatter | solution.py:31
  83.4 1.9 copy-start.1
  83.4 218.0 %all-reduce.3.cloned.1.call-start = ((), (), s32[]{:S(2)}) async-start(), calls=%async_computation.4 | async-start | bytes 262144 | tf_op jit(solution)/shard_map/psum | solution.py:32
  186.0 750.1 %all-gather.2.cloned.1.call-start = ((), (), s32[]{:S(2)}) async-start(), calls=%async_computation.5 | async-start | bytes 2162688 | tf_op jit(solution)/shard_map/all_gather | solution.py:47
  301.4 564.0 %copy-start = (f32[32,1024]{1,0:T(8,128)S(1)}, f32[32,1024]{1,0:T(8,128)}, u32[]{:S(2)}) copy-start(f32[32,1024]{1,0:T(8,128)} %all-reduce.3.cloned.1.call-done) | copy-start | bytes 393220
  402.4 46.0 %copy-start.2 = (f32[32]{0:T(128)}, f32[32]{0:T(128)S(1)}, u32[]{:S(2)}) copy-start(f32[32]{0:T(128)S(1)} %fusion.24) | copy-start | bytes 388 | tf_op jit(solution)/shard_map/while
  448.7 46.0 %copy-start.2 = (f32[32]{0:T(128)}, f32[32]{0:T(128)S(1)}, u32[]{:S(2)}) copy-start(f32[32]{0:T(128)S(1)} %fusion.24) | copy-start | bytes 388 | tf_op jit(solution)/shard_map/while
  494.9 46.0 %copy-start.2 = (f32[32]{0:T(128)}, f32[32]{0:T(128)S(1)}, u32[]{:S(2)}) copy-start(f32[32]{0:T(128)S(1)} %fusion.24) | copy-start | bytes 388 | tf_op jit(solution)/shard_map/while
  541.2 46.0 %copy-start.2 = (f32[32]{0:T(128)}, f32[32]{0:T(128)S(1)}, u32[]{:S(2)}) copy-start(f32[32]{0:T(128)S(1)} %fusion.24) | copy-start | bytes 388 | tf_op jit(solution)/shard_map/while
  587.4 46.0 %copy-start.2 = (f32[32]{0:T(128)}, f32[32]{0:T(128)S(1)}, u32[]{:S(2)}) copy-start(f32[32]{0:T(128)S(1)} %fusion.24) | copy-start | bytes 388 | tf_op jit(solution)/shard_map/while
  633.7 46.0 %copy-start.2 = (f32[32]{0:T(128)}, f32[32]{0:T(128)S(1)}, u32[]{:S(2)}) copy-start(f32[32]{0:T(128)S(1)} %fusion.24) | copy-start | bytes 388 | tf_op jit(solution)/shard_map/while
  680.0 46.0 %copy-start.2 = (f32[32]{0:T(128)}, f32[32]{0:T(128)S(1)}, u32[]{:S(2)}) copy-start(f32[32]{0:T(128)S(1)} %fusion.24) | copy-start | bytes 388 | tf_op jit(solution)/shard_map/while
  726.2 46.0 %copy-start.2 = (f32[32]{0:T(128)}, f32[32]{0:T(128)S(1)}, u32[]{:S(2)}) copy-start(f32[32]{0:T(128)S(1)} %fusion.24) | copy-start | bytes 388 | tf_op jit(solution)/shard_map/while
  772.5 46.0 %copy-start.2 = (f32[32]{0:T(128)}, f32[32]{0:T(128)S(1)}, u32[]{:S(2)}) copy-start(f32[32]{0:T(128)S(1)} %fusion.24) | copy-start | bytes 388 | tf_op jit(solution)/shard_map/while
  818.7 46.0 %copy-start.2 = (f32[32]{0:T(128)}, f32[32]{0:T(128)S(1)}, u32[]{:S(2)}) copy-start(f32[32]{0:T(128)S(1)} %fusion.24) | copy-start | bytes 388 | tf_op jit(solution)/shard_map/while
Sparse Core Ops, SparseCore 0:
  83.5 102.4 reduce-scatter.1
  189.2 112.2 all-reduce.2
  866.3 69.8 all-gather.1
where the time goes:
time: 1010 us
  blocking collectives  690 us (68%)
  waiting for transfers between devices  283 us (28%)
  between operations  14.4 us (1%)
  matrix products  10.1 us (1%)
    psum x10, blocking collectives, column_total(): return lax.psum(values, 'mem')  458 us
    psum x1, waiting for transfers between devices, per_device(): gram_rows = lax.psum(local_rows, 'space')  114 us
    reduce_scatter x1, waiting for transfers between devices, per_device(): lax.psum_scatter(partial_gram, 'mem', scatter_dimension=0, tiled=True)  98.8 us
    all_to_all x1, blocking collectives, per_device(): lax.all_to_all(ensemble, 'mem', split_axis=1, concat_axis=0, tiled=True)  72.3 us
    all_gather x1, waiting for transfers between devices, per_device(): coupling = lax.all_gather(coupling_rows, 'mem', axis=0, tiled=True)  70 us
    all_to_all x1, blocking collectives, per_device(): return lax.all_to_all(mixed, 'mem', split_axis=0, concat_axis=1, tiled=True)  63.8 us
    unnamed x1, blocking collectives  48.6 us
    psum x1, blocking collectives, per_device(): dist_total = lax.psum(jnp.sum(dist), 'mem')  47.1 us
  transfers between devices with their start and end apart: 3, of which 3 were waited for; matrix products, arithmetic and copies ran while one was open for 0% of the time, Pallas kernels for 0%

commit v1 on v0

--- a/solution.py
+++ b/solution.py
@@ -44,7 +44,9 @@
         return lax.psum(values, "mem")
 
     coupling_rows = coupling_from(kernel, weights_rows, column_total)
-    coupling = lax.all_gather(coupling_rows, "mem", axis=0, tiled=True)
+    coupling = jnp.concatenate(
+        lax.all_to_all(jnp.stack([coupling_rows] * lax.axis_size("mem")), "mem", 0, 0), axis=0
+    )
     mixed = lax.dot_general(
         coupling, relaid, (((0,), (0,)), ((), ())), preferred_element_type=jnp.float32
     )

time: 1010 us -> 1050 us (1.040)
  blocking collectives: 690 us -> 797 us
  waiting for transfers between devices: 283 us -> 213 us
    all_to_all x0 -> x1, blocking collectives: none -> 112 us  [per_device(): lax.all_to_all(jnp.stack([coupling_rows] * lax.axis_size('mem')), 'mem',...]
    all_gather x1 -> x0, waiting for transfers between devices: 70 us -> none  [per_device(): coupling = lax.all_gather(coupling_rows, 'mem', axis=0, tiled=True)]
  transfers between devices with their start and end apart: 3 -> 2, of which waited for: 3 -> 2; matrix products, arithmetic and copies ran while one was open for 0% -> 0% of each run, Pallas kernels for 0% -> 0%
where the time goes in v1:
time: 1050 us
  blocking collectives  797 us (76%)
  waiting for transfers between devices  213 us (20%)
  between operations  14.7 us (1%)
    psum x10, blocking collectives, column_total(): return lax.psum(values, 'mem')  458 us
    psum x1, waiting for transfers between devices, per_device(): gram_rows = lax.psum(local_rows, 'space')  114 us
    all_to_all x1, blocking collectives, per_device(): lax.all_to_all(jnp.stack([coupling_rows] * lax.axis_size('mem')), 'mem',...  112 us
    reduce_scatter x1, waiting for transfers between devices, per_device(): lax.psum_scatter(partial_gram, 'mem', scatter_dimension=0, tiled=True)  98.8 us
    all_to_all x1, blocking collectives, per_device(): lax.all_to_all(ensemble, 'mem', split_axis=1, concat_axis=0, tiled=True)  72.3 us
    all_to_all x1, blocking collectives, per_device(): return lax.all_to_all(mixed, 'mem', split_axis=0, concat_axis=1, tiled=True)  59 us
    unnamed x1, blocking collectives  48.6 us
    psum x1, blocking collectives, per_device(): dist_total = lax.psum(jnp.sum(dist), 'mem')  47.1 us
  transfers between devices with their start and end apart: 2, of which 2 were waited for; matrix products, arithmetic and copies ran while one was open for 0% of the time, Pallas kernels for 0%

profile of v1, /device:TPU:1, one launch (start us, length us, event | category | flops | bytes accessed | tf_op | source)
XLA Modules:
  0.0 1045.6 jit_solution(998897535589940340)
XLA Ops:
  6.5 1.4 copy.9
  7.9 72.3 %all_to_all.43 = bf16[32,32,512]{2,0,1:T(8,128)(2,1)S(1)} all-to-all(bf16[32,32,512]{2,0,1:T(8,128)(2,1)S(1)} %bitcast.46), channel_id=1, replica_groups=mesh['mem'=32,'space'=16] {'mem'}, dimensions={1} | all-to-all | bytes 2097152 | tf_op jit(solution)/shard_map/all_to_all | solution.py:26
  80.2 3.2 fusion.7
  83.5 1.3 dynamic-slice
  85.3 0.6 reduce_max.9
  85.9 1.2 fusion.6
  87.2 98.8 %reduce-scatter.2.cloned.1.call-done = f32[32,1024]{1,0:T(8,128)} async-done(((f32[1024,1024]{1,0:T(8,128)}), f32[32,1024]{1,0:T(8,128)}) %reduce-scatter.2.cloned.1.call-update) | async-done | bytes 131088 | tf_op jit(solution)/shard_map/reduce_scatter | solution.py:31
  186.0 1.2 fusion.5
  187.3 114.1 %all-reduce.3.cloned.1.call-done = f32[32,1024]{1,0:T(8,128)} async-done(((f32[32,1024]{1,0:T(8,128)}), f32[32,1024]{1,0:T(8,128)}) %all-reduce.3.cloned.1.call-update) | async-done | bytes 131088 | tf_op jit(solution)/shard_map/psum | solution.py:32
  301.4 1.0 select_reduce_fusion
  302.4 0.2 dynamic-update-slice
  302.7 48.6 %all-reduce = f32[1024]{0:T(1024)S(1)} all-reduce(f32[1024]{0:T(1024)S(1)} %dynamic-update-slice), channel_id=1, replica_groups=mesh['mem'=32,'space'=16] {'mem'}, use_global_device_ids=true, to_apply=%add | all-reduce | flops 1024 | bytes 8192
  351.2 1.7 fusion.4
  352.9 0.5 copy.13
  353.4 47.1 %psum.22 = f32[]{:T(128)} all-reduce(f32[]{:T(128)} %fusion.4), channel_id=1, replica_groups=mesh['mem'=32,'space'=16] {'mem'}, use_global_device_ids=true, to_apply=%region_6.0 | all-reduce | flops 1 | bytes 8 | tf_op jit(solution)/shard_map/psum | solution.py:38
  401.2 1.0 divide_exponential_fusion
  402.2 462.6 %while.13 = (s32[]{:T(128)}, f32[32]{0:T(128)}, f32[1024]{0:T(1024)S(1)}, f32[32,1024]{1,0:T(8,128)S(1)}, f32[32]{0:T(128)S(1)}, /*index=5*/s32[]{:T(128)}, s32[]{:T(128)}) while((s32[]{:T(128)}, f32[32]{0:T(128)}, f32[1024]{0:T(1024)S(1)}, f32[32,1024]{1,0:T(8,128)S(1)}, f32[32]{0:T(128)S(1)}, /*index=5*/s32[]{:T(128)}, ...), condition=%wide.region_9.0_spmd.clone, body=%wide.region_7.0_spmd.clone.sunk | while | flops 789539 | bytes 295923 | solution.py:19
  402.2 0.2 fusion.24
  402.4 0.2 fusion.25
  402.6 45.8 %psum.25 = f32[1024]{0:T(1024)S(1)} all-reduce(f32[1024]{0:T(1024)S(1)} %bitcast.51), channel_id=1, replica_groups=mesh['mem'=32,'space'=16] {'mem'}, use_global_device_ids=true, to_apply=%region_8.0 | all-reduce | flops 1024 | bytes 8192 | tf_op jit(solution)/shard_map/while/body/eval_jaxpr/psum | solution.py:44
  448.7 0.2 fusion.25
  448.9 45.8 %psum.25 = f32[1024]{0:T(1024)S(1)} all-reduce(f32[1024]{0:T(1024)S(1)} %bitcast.51), channel_id=1, replica_groups=mesh['mem'=32,'space'=16] {'mem'}, use_global_device_ids=true, to_apply=%region_8.0 | all-reduce | flops 1024 | bytes 8192 | tf_op jit(solution)/shard_map/while/body/eval_jaxpr/psum | solution.py:44
  494.7 0.2 fusion.24
  494.9 0.2 fusion.25
  495.2 45.8 %psum.25 = f32[1024]{0:T(1024)S(1)} all-reduce(f32[1024]{0:T(1024)S(1)} %bitcast.51), channel_id=1, replica_groups=mesh['mem'=32,'space'=16] {'mem'}, use_global_device_ids=true, to_apply=%region_8.0 | all-reduce | flops 1024 | bytes 8192 | tf_op jit(solution)/shard_map/while/body/eval_jaxpr/psum | solution.py:44
  541.0 0.2 fusion.24
  541.2 0.2 fusion.25
  541.4 45.8 %psum.25 = f32[1024]{0:T(1024)S(1)} all-reduce(f32[1024]{0:T(1024)S(1)} %bitcast.51), channel_id=1, replica_groups=mesh['mem'=32,'space'=16] {'mem'}, use_global_device_ids=true, to_apply=%region_8.0 | all-reduce | flops 1024 | bytes 8192 | tf_op jit(solution)/shard_map/while/body/eval_jaxpr/psum | solution.py:44
  587.4 0.2 fusion.25
  587.7 45.8 %psum.25 = f32[1024]{0:T(1024)S(1)} all-reduce(f32[1024]{0:T(1024)S(1)} %bitcast.51), channel_id=1, replica_groups=mesh['mem'=32,'space'=16] {'mem'}, use_global_device_ids=true, to_apply=%region_8.0 | all-reduce | flops 1024 | bytes 8192 | tf_op jit(solution)/shard_map/while/body/eval_jaxpr/psum | solution.py:44
  633.5 0.2 fusion.24
  633.7 0.2 fusion.25
  633.9 45.8 %psum.25 = f32[1024]{0:T(1024)S(1)} all-reduce(f32[1024]{0:T(1024)S(1)} %bitcast.51), channel_id=1, replica_groups=mesh['mem'=32,'space'=16] {'mem'}, use_global_device_ids=true, to_apply=%region_8.0 | all-reduce | flops 1024 | bytes 8192 | tf_op jit(solution)/shard_map/while/body/eval_jaxpr/psum | solution.py:44
  679.8 0.2 fusion.24
  680.0 0.2 fusion.25
  680.2 45.8 %psum.25 = f32[1024]{0:T(1024)S(1)} all-reduce(f32[1024]{0:T(1024)S(1)} %bitcast.51), channel_id=1, replica_groups=mesh['mem'=32,'space'=16] {'mem'}, use_global_device_ids=true, to_apply=%region_8.0 | all-reduce | flops 1024 | bytes 8192 | tf_op jit(solution)/shard_map/while/body/eval_jaxpr/psum | solution.py:44
  726.2 0.2 fusion.25
  726.5 45.8 %psum.25 = f32[1024]{0:T(1024)S(1)} all-reduce(f32[1024]{0:T(1024)S(1)} %bitcast.51), channel_id=1, replica_groups=mesh['mem'=32,'space'=16] {'mem'}, use_global_device_ids=true, to_apply=%region_8.0 | all-reduce | flops 1024 | bytes 8192 | tf_op jit(solution)/shard_map/while/body/eval_jaxpr/psum | solution.py:44
  772.5 0.2 fusion.25
  772.7 45.8 %psum.25 = f32[1024]{0:T(1024)S(1)} all-reduce(f32[1024]{0:T(1024)S(1)} %bitcast.51), channel_id=1, replica_groups=mesh['mem'=32,'space'=16] {'mem'}, use_global_device_ids=true, to_apply=%region_8.0 | all-reduce | flops 1024 | bytes 8192 | tf_op jit(solution)/shard_map/while/body/eval_jaxpr/psum | solution.py:44
  818.7 0.2 fusion.25
  819.0 45.8 %psum.25 = f32[1024]{0:T(1024)S(1)} all-reduce(f32[1024]{0:T(1024)S(1)} %bitcast.51), channel_id=1, replica_groups=mesh['mem'=32,'space'=16] {'mem'}, use_global_device_ids=true, to_apply=%region_8.0 | all-reduce | flops 1024 | bytes 8192 | tf_op jit(solution)/shard_map/while/body/eval_jaxpr/psum | solution.py:44
  864.8 0.6 broadcast_multiply_fusion
  865.5 0.2 stack.2
  865.8 111.6 %all_to_all.44 = bf16[32,32,1024]{2,1,0:T(8,128)(2,1)S(1)} all-to-all(bf16[32,32,1024]{2,1,0:T(8,128)(2,1)S(1)} %stack.2), channel_id=1, replica_groups=mesh['mem'=32,'space'=16] {'mem'}, dimensions={0} | all-to-all | bytes 4194304 | tf_op jit(solution)/shard_map/all_to_all | solution.py:48
  977.4 1.3 bitcast_convert_fusion
  978.7 59.0 %all_to_all.45 = bf16[32,32,512]{2,1,0:T(8,128)(2,1)S(1)} all-to-all(bf16[32,32,512]{2,1,0:T(8,128)(2,1)S(1)} %bitcast.49), channel_id=1, replica_groups=mesh['mem'=32,'space'=16] {'mem'}, dimensions={0} | all-to-all | bytes 2097152 | tf_op jit(solution)/shard_map/all_to_all | solution.py:54
  1037.7 1.1 copy.7
  (57 shorter events, 1.3 us)
Async XLA Ops:
  6.5 179.5 %reduce-scatter.2.cloned.1.call-start = ((), (), s32[]{:S(2)}) async-start(), calls=%async_computation.4 | async-start | bytes 4325376 | tf_op jit(solution)/shard_map/reduce_scatter | solution.py:31
  83.4 1.9 copy-start.1
  83.4 218.0 %all-reduce.3.cloned.1.call-start = ((), (), s32[]{:S(2)}) async-start(), calls=%async_computation.5 | async-start | bytes 262144 | tf_op jit(solution)/shard_map/psum | solution.py:32
  301.4 564.0 %copy-start = (f32[32,1024]{1,0:T(8,128)S(1)}, f32[32,1024]{1,0:T(8,128)}, u32[]{:S(2)}) copy-start(f32[32,1024]{1,0:T(8,128)} %all-reduce.3.cloned.1.call-done) | copy-start | bytes 393220
  402.4 46.0 %copy-start.2 = (f32[32]{0:T(128)}, f32[32]{0:T(128)S(1)}, u32[]{:S(2)}) copy-start(f32[32]{0:T(128)S(1)} %fusion.24) | copy-start | bytes 388 | tf_op jit(solution)/shard_map/while
  448.7 46.0 %copy-start.2 = (f32[32]{0:T(128)}, f32[32]{0:T(128)S(1)}, u32[]{:S(2)}) copy-start(f32[32]{0:T(128)S(1)} %fusion.24) | copy-start | bytes 388 | tf_op jit(solution)/shard_map/while
  494.9 46.0 %copy-start.2 = (f32[32]{0:T(128)}, f32[32]{0:T(128)S(1)}, u32[]{:S(2)}) copy-start(f32[32]{0:T(128)S(1)} %fusion.24) | copy-start | bytes 388 | tf_op jit(solution)/shard_map/while
  541.2 46.0 %copy-start.2 = (f32[32]{0:T(128)}, f32[32]{0:T(128)S(1)}, u32[]{:S(2)}) copy-start(f32[32]{0:T(128)S(1)} %fusion.24) | copy-start | bytes 388 | tf_op jit(solution)/shard_map/while
  587.4 46.0 %copy-start.2 = (f32[32]{0:T(128)}, f32[32]{0:T(128)S(1)}, u32[]{:S(2)}) copy-start(f32[32]{0:T(128)S(1)} %fusion.24) | copy-start | bytes 388 | tf_op jit(solution)/shard_map/while
  633.7 46.0 %copy-start.2 = (f32[32]{0:T(128)}, f32[32]{0:T(128)S(1)}, u32[]{:S(2)}) copy-start(f32[32]{0:T(128)S(1)} %fusion.24) | copy-start | bytes 388 | tf_op jit(solution)/shard_map/while
  680.0 46.0 %copy-start.2 = (f32[32]{0:T(128)}, f32[32]{0:T(128)S(1)}, u32[]{:S(2)}) copy-start(f32[32]{0:T(128)S(1)} %fusion.24) | copy-start | bytes 388 | tf_op jit(solution)/shard_map/while
  726.2 46.0 %copy-start.2 = (f32[32]{0:T(128)}, f32[32]{0:T(128)S(1)}, u32[]{:S(2)}) copy-start(f32[32]{0:T(128)S(1)} %fusion.24) | copy-start | bytes 388 | tf_op jit(solution)/shard_map/while
  772.5 46.0 %copy-start.2 = (f32[32]{0:T(128)}, f32[32]{0:T(128)S(1)}, u32[]{:S(2)}) copy-start(f32[32]{0:T(128)S(1)} %fusion.24) | copy-start | bytes 388 | tf_op jit(solution)/shard_map/while
  818.7 46.0 %copy-start.2 = (f32[32]{0:T(128)}, f32[32]{0:T(128)S(1)}, u32[]{:S(2)}) copy-start(f32[32]{0:T(128)S(1)} %fusion.24) | copy-start | bytes 388 | tf_op jit(solution)/shard_map/while
Sparse Core Ops, SparseCore 0:
  83.5 102.4 reduce-scatter.1
  189.2 112.2 all-reduce.2
